TPU v7x, 32 devices: a whole 2x2x4 slice. The times are simulated.
32 devices in a mesh: grp: 4 (over x, core), blk: 8 (over z, y).
Axes of the slice: x: 2, y: 2, z: 4, core: 2. Of those that a mesh axis runs over, the one named last changes fastest.
Arguments:
- vector: bfloat16 [32, 128], P(('grp', 'blk')), may hold values from -6 to 6
- integrals: bfloat16 [1024, 500, 500], P(('grp', 'blk')), may hold values from -0.072 to 0.072
- orbitals: bfloat16 [26, 500], replicated, may hold values from -0.25 to 0.25
- alpha_addr: int32 [32, 676], replicated, may hold values from 0 to 31
- alpha_sign: int32 [32, 676], replicated, may hold values from -1 to 1
- beta_addr: int32 [128, 676], replicated, may hold values from 0 to 127
- beta_sign: int32 [128, 676], replicated, may hold values from -1 to 1
- seg_alpha: int32 [32], replicated, may hold values from 0 to 9, never falling along the last dimension, each value on 1 to 6 neighbouring positions
- seg_beta: int32 [128], replicated, may hold values from 0 to 9, never falling along the last dimension, each value on 1 to 25 neighbouring positions
- allowed: int32 [10, 10], replicated, may hold values 0 or 1
Outputs:
- sigma_t: float32 [128, 32], P(('grp', 'blk'))
All inputs are finite; a program needn't handle non-finite values.
Results may differ from a plain program's by a relative error of at most 0.0056.
Values may be sent and summed in bfloat16 or wider, within the bound.
No kernel may reach another device: no remote copies, remote signals or barrier semaphores. Data moves between devices by JAX's collectives and lax.ppermute only.
A program may use at most 64 MiB of HBM per device.

v0:
```python
import jax
import jax.numpy as jnp
from jax import lax
from jax.sharding import PartitionSpec as P


def onehot(segment_ids, count):
    return (segment_ids[:, None] == jnp.arange(count, dtype=jnp.int32)[None, :]).astype(jnp.float32)


def on_device(
    vector,
    integrals,
    orbitals,
    alpha_addr,
    alpha_sign,
    beta_addr,
    beta_sign,
    seg_alpha,
    seg_beta,
    allowed,
):
    devices = lax.axis_size(("grp", "blk"))
    position = lax.axis_index(("grp", "blk"))
    a_rows = vector.shape[0]
    n_beta = vector.shape[1]
    n_alpha = a_rows * devices
    b_cols = n_beta // devices
    pair_count = alpha_addr.shape[1]
    orbital_count = orbitals.shape[0]
    block_count = allowed.shape[0]
    allowed_f = allowed.astype(jnp.float32)
    local_alpha = lax.dynamic_slice_in_dim(seg_alpha, position * a_rows, a_rows)
    row_mask = jnp.dot(
        jnp.dot(onehot(local_alpha, block_count), allowed_f, precision=lax.Precision.HIGHEST),
        onehot(seg_beta, block_count).T,
        precision=lax.Precision.HIGHEST,
    )
    masked = (vector.astype(jnp.float32) * row_mask).astype(jnp.bfloat16)
    masked_t = masked.T
    half_done = jnp.einsum(
        "jn,pmn->pjm", orbitals, integrals, preferred_element_type=jnp.float32
    ).astype(jnp.bfloat16)
    factors = (
        jnp.einsum("im,pjm->pij", orbitals, half_done, preferred_element_type=jnp.float32)
        .reshape(-1, pair_count)
        .astype(jnp.bfloat16)
    )
    factor_piece = lax.all_gather(factors, ("grp", "blk"), axis=0, tiled=True)
    coulomb = lax.dot_general(
        factor_piece, factor_piece, (((0,), (0,)), ((), ())), preferred_element_type=jnp.float32
    ).astype(jnp.bfloat16)
    whole_t = lax.all_gather(masked_t, ("grp", "blk"), axis=1, tiled=True)
    local_addr = lax.dynamic_slice_in_dim(beta_addr, position * b_cols, b_cols)
    local_sign = lax.dynamic_slice_in_dim(beta_sign, position * b_cols, b_cols)
    picked_rows = jnp.take(whole_t, local_addr.reshape(-1), axis=0).reshape(
        local_addr.shape[0], pair_count, whole_t.shape[1]
    )
    products = jnp.einsum(
        "uv,bva->bua",
        coulomb,
        picked_rows * local_sign.astype(jnp.bfloat16)[:, :, None],
        preferred_element_type=jnp.float32,
    ).astype(jnp.bfloat16)
    addr_blocks = alpha_addr.reshape(n_alpha, orbital_count, orbital_count).transpose(1, 2, 0)
    sign_blocks = alpha_sign.reshape(n_alpha, orbital_count, orbital_count).transpose(1, 2, 0)
    product_blocks = products.reshape(b_cols, orbital_count, orbital_count, n_alpha).transpose(
        1, 0, 2, 3
    )
    targets = jnp.arange(n_alpha, dtype=jnp.int32)

    def add_block(total, pieces):
        addr_piece, sign_piece, product_piece = pieces
        table = jnp.where(
            addr_piece[:, :, None] == targets[None, None, :],
            sign_piece.astype(jnp.bfloat16)[:, :, None],
            jnp.zeros((), jnp.bfloat16),
        )
        return (
            total
            + jnp.einsum("jaz,bjz->ba", table, product_piece, preferred_element_type=jnp.float32),
            None,
        )

    sigma_rows = lax.scan(
        add_block,
        jnp.zeros((b_cols, n_alpha), jnp.float32),
        (addr_blocks, sign_blocks, product_blocks),
    )[0]
    local_beta = lax.dynamic_slice_in_dim(seg_beta, position * b_cols, b_cols)
    column_mask = jnp.dot(
        jnp.dot(onehot(local_beta, block_count), allowed_f.T, precision=lax.Precision.HIGHEST),
        onehot(seg_alpha, block_count).T,
        precision=lax.Precision.HIGHEST,
    )
    return sigma_rows * column_mask


def solution(mesh):
    placed = (
        P(("grp", "blk"), None),
        P(("grp", "blk"), None, None),
        P(),
        P(),
        P(),
        P(),
        P(),
        P(),
        P(),
        P(),
    )
    return jax.shard_map(
        on_device, mesh=mesh, in_specs=placed, out_specs=P(("grp", "blk"), None), check_vma=False
    )
```

profile of v0, /device:TPU:0, one launch (start us, length us, event | category | flops | bytes accessed | tf_op | source)
XLA Modules:
  0.0 144.5 jit_solution(4271699657112543657)
XLA Ops:
  6.5 24.0 %fusion.27 = bf16[32,26,26]{1,2,0:T(8,128)(2,1)S(1)} fusion(bf16[32,500,500]{2,0,1:T(8,128)(2,1)} %param.13, bf16[26,500]{1,0:T(8,128)(2,1)} %param.14), kind=kOutput, calls=%fused_computation.25 | convolution fusion | flops 438069632 | bytes 16069264 | tf_op jit(solution)/shard_map/im,pjm->pij/dot_general | solution.py:45
  30.6 0.3 copy.46
  30.9 0.9 convert_element_type.58
  31.9 0.2 compare_and_fusion
  32.4 0.6 dynamic_slice.24
  33.0 0.7 convolution_bitcast_fusion.1
  33.7 0.2 fusion.32
  33.9 70.0 %all-gather = bf16[32,1,128]{2,1,0:T(2,128)(2,1)S(1)} all-gather(bf16[1,1,128]{2,1,0:T(2,128)(2,1)S(1)} %fusion.32), channel_id=1, replica_groups=mesh['grp'=4,'blk'=8] {'grp','blk'}, dimensions={0}, use_global_device_ids=true | all-gather | bytes 8448 | tf_op jit(solution)/shard_map/all_gather | solution.py:53
  104.1 5.8 %gather_fusion = bf16[2704,32]{1,0:T(8,128)(2,1)S(1)} fusion(bf16[128,32]{1,0:T(8,128)(2,1)S(1)} %bitcast.62, s32[3072]{0:T(1024)S(1)} %pad_clamp_fusion), kind=kCustom, calls=%fused_computation | custom fusion | bytes 356928 | tf_op jit(solution)/shard_map/jit(_take)/gather | solution.py:56
  110.0 0.3 copy.43
  110.2 0.3 gather.7
  110.5 0.2 copy.40
  110.7 0.2 constant_dynamic-slice_fusion.2
  110.9 0.2 copy.53
  111.0 0.5 reshape.80
  111.5 0.5 reshape.81
  112.0 0.2 fusion.39
  112.4 3.8 %fusion.30 = bf16[4,676,32]{1,2,0:T(8,128)(2,1)S(1)} fusion(bf16[1024,676]{1,0:T(8,128)(2,1)} %all-gather.3.cloned.1.call-done, bf16[4,676,32]{1,0,2:T(4,128)(2,1)S(1)} %select_multiply_fusion), kind=kOutput, calls=%fused_computation.26 | convolution fusion | flops 1053416192 | bytes 1730560 | tf_op jit(solution)/shard_map/uv,bva->bua/dot_general | solution.py:59
  116.2 2.2 %reshape.79 = bf16[4,26,26,32]{2,1,3,0:T(8,128)(2,1)S(1)} reshape(bf16[4,676,32]{1,2,0:T(8,128)(2,1)S(1)} %fusion.30) | data formatting | bytes 346112 | tf_op jit(solution)/shard_map/reshape | solution.py:67
  118.4 1.8 %copy.48 = bf16[26,4,26,32]{3,1,2,0:T(4,128)(2,1)S(1)} copy(bf16[26,4,26,32]{2,0,3,1:T(8,128)(2,1)S(1)} %bitcast.63) | data formatting | bytes 346112
  120.2 16.6 %while.11 = (s32[]{:T(128)}, f32[4,32]{1,0:T(4,128)S(1)}, bf16[26,4,26,32]{3,1,2,0:T(4,128)(2,1)S(1)}, s32[26,26,32]{1,0,2:T(8,128)S(1)}, s32[26,26,32]{1,0,2:T(8,128)S(1)}, /*index=5*/s32[]{:T(128)}, s32[]{:T(128)}) while((s32[]{:T(128)}, f32[4,32]{1,0:T(4,128)S(1)}, bf16[26,4,26,32]{3,1,2,0:T(4,128)(2,1)S(1)}, ...), condition=%wide.region_1.2_spmd.clone, body=%wide.region_0.1_spmd.clone.sunk | while | flops 267331 | bytes 85471 | solution.py:85
  120.5 0.4 fusion.56
  121.1 0.4 fusion.56
  121.7 0.4 fusion.56
  122.4 0.4 fusion.56
  123.0 0.4 fusion.56
  123.7 0.4 fusion.56
  124.3 0.4 fusion.56
  124.9 0.4 fusion.56
  125.6 0.4 fusion.56
  126.2 0.4 fusion.56
  126.9 0.4 fusion.56
  127.5 0.4 fusion.56
  128.1 0.4 fusion.56
  128.8 0.4 fusion.56
  129.4 0.4 fusion.56
  130.0 0.4 fusion.56
  130.7 0.4 fusion.56
  131.3 0.4 fusion.56
  132.0 0.4 fusion.56
  132.6 0.4 fusion.56
  133.2 0.4 fusion.56
  133.9 0.4 fusion.56
  134.5 0.4 fusion.56
  135.2 0.4 fusion.56
  135.8 0.4 fusion.56
  136.4 0.4 fusion.56
  136.9 0.8 convolution_multiply_fusion
  (132 shorter events, 6.5 us)
Async XLA Ops:
  6.5 104.1 %copy-start = (s32[128,676]{0,1:T(8,128)S(1)}, s32[128,676]{0,1:T(8,128)}, u32[]{:S(2)}) copy-start(s32[128,676]{0,1:T(8,128)} %param.18) | copy-start | bytes 1038340
  6.5 25.4 %copy-start.1 = (s32[128,676]{0,1:T(8,128)S(1)}, s32[128,676]{0,1:T(8,128)}, u32[]{:S(2)}) copy-start(s32[128,676]{0,1:T(8,128)} %param.17) | copy-start | bytes 1038340
  6.5 105.8 %all-gather.3.cloned.1.call-start = ((), (), s32[]{:S(2)}) async-start(), calls=%async_computation | async-start | bytes 1622016 | tf_op jit(solution)/shard_map/all_gather | solution.py:49
  30.5 1.8 %copy-start.5 = (s32[128]{0:T(128)S(1)}, s32[128]{0:T(128)}, u32[]{:S(2)}) copy-start(s32[128]{0:T(128)} %param.20) | copy-start | bytes 1540
  30.5 1.9 %copy-start.7 = (s32[32]{0:T(128)S(1)}, s32[32]{0:T(128)}, u32[]{:S(2)}) copy-start(s32[32]{0:T(128)} %param.19) | copy-start | bytes 388
  30.5 2.5 %copy-start.4 = (s32[10,10]{1,0:T(8,128)S(1)}, s32[10,10]{1,0:T(8,128)}, u32[]{:S(2)}) copy-start(s32[10,10]{1,0:T(8,128)} %param.21) | copy-start | bytes 1204
  30.6 3.2 %copy-start.6 = (bf16[1,128]{1,0:T(2,128)(2,1)S(1)}, bf16[1,128]{1,0:T(2,128)(2,1)}, u32[]{:S(2)}) copy-start(bf16[1,128]{1,0:T(2,128)(2,1)} %param.12) | copy-start | bytes 772
  109.9 1.1 copy-start.2
  110.0 1.6 %copy-start.3 = (s32[32,676]{1,0:T(8,128)S(1)}, s32[32,676]{1,0:T(8,128)}, u32[]{:S(2)}) copy-start(s32[32,676]{1,0:T(8,128)} %param.16) | copy-start | bytes 259588
Sparse Core Ops, SparseCore 0:
  32.0 57.7 all-gather.2
where the time goes:
time: 145 us; the launch traced here: 144 us
  blocking collectives  70 us (48%)
  matrix products  40.3 us (28%)
  local copies, waits for them, and re-layouts  19.7 us (14%)
  between operations  13.6 us (9%)
    all_gather x1, blocking collectives, on_device(): whole_t = lax.all_gather(masked_t, ('grp', 'blk'), axis=1, tiled=True)  70 us
    dot_general x1, matrix products, on_device(): jnp.einsum('im,pjm->pij', orbitals, half_done, preferred_element_type=jnp...  24 us
    dot_general x26, matrix products, add_block(): jnp.einsum('jaz,bjz->ba', table, product_piece, preferred_element_type=jn...  10.6 us
    gather x3, local copies, waits for them, and re-layouts, on_device(): jnp.take(whole_t, local_addr.reshape(-1), axis=0)  6.33 us
    dynamic_slice x78, local copies, waits for them, and re-layouts, on_device(): lax.scan(add_block, jnp.zeros((b_cols, n_alpha), jnp.float32), (addr_bloc...  5.56 us
    dot_general x1, matrix products, on_device(): jnp.einsum('uv,bva->bua', coulomb, picked_rows * local_sign.astype(jnp.bf...  3.83 us
  transfers between devices with their start and end apart: 1, of which 0 were waited for; matrix products, arithmetic and copies ran while one was open for 7% of the time, Pallas kernels for 0%

commit v1 on v0

v1 whole, which is shorter than its diff:
```python
import functools

import jax
import jax.numpy as jnp
from jax import lax
from jax.experimental import pallas as pl
from jax.experimental.pallas import tpu as pltpu
from jax.sharding import PartitionSpec as P

AXES = ("grp", "blk")
LANES = 128
SUBLANES = 8
PACK = 16
NT = (((1,), (1,)), ((), ()))


def transform_kernel(low_ref, high_ref, orb_ref, out_ref, half_ref, turn_ref, flat_ref, *, rows, half, stride):
    norb = orb_ref.shape[0]
    groups = low_ref.shape[1] // PACK
    step = pl.program_id(0)
    weights = orb_ref[...]
    total = None
    for side, block_ref in enumerate((low_ref, high_ref)):
        for group in range(groups):
            place = (side * groups + group) * 32
            pieces = []
            if place:
                pieces.append(jnp.zeros((place, weights.shape[1]), jnp.bfloat16))
            pieces.append(weights)
            pieces.append(jnp.zeros((LANES - place - norb, weights.shape[1]), jnp.bfloat16))
            placed = jnp.concatenate(pieces, axis=0)
            block = block_ref[:, group * PACK : (group + 1) * PACK, :].reshape(rows * PACK, block_ref.shape[2])
            part = lax.dot_general(block, placed, NT, preferred_element_type=jnp.float32)
            total = part if total is None else total + part
    for row in range(rows):
        half_ref[pl.ds(step * rows + row, PACK, stride=stride), :] = total[row * PACK : (row + 1) * PACK, :]

    @pl.when(step == pl.num_programs(0) - 1)
    def _():
        first = weights[:, :half]
        second = weights[:, half : 2 * half]
        for r in range(PACK):
            right = half_ref[r * stride : r * stride + half, :].astype(jnp.bfloat16)
            a = jnp.dot(first, right, preferred_element_type=jnp.float32)
            b = jnp.dot(second, right, preferred_element_type=jnp.float32)
            turn_ref[pl.ds(r, norb, stride=PACK), :] = a + pltpu.roll(b, LANES - groups * 32, 1)
        for i in range(norb):
            piece = turn_ref[i * PACK : (i + 1) * PACK, :]
            for group in range(groups):
                flat_ref[group * PACK : (group + 1) * PACK, i * norb : (i + 1) * norb] = piece[
                    :, group * 32 : group * 32 + norb
                ]
        out_ref[...] = flat_ref[...].astype(jnp.bfloat16)


def transform(integrals, orbitals):
    aux, nbas, _ = integrals.shape
    norb = orbitals.shape[0]
    half = nbas // 2
    if aux % PACK or (aux // PACK) * 64 != LANES or norb > 32 or nbas % 2:
        half_done = jnp.einsum("jn,pmn->pjm", orbitals, integrals, preferred_element_type=jnp.float32).astype(
            jnp.bfloat16
        )
        return (
            jnp.einsum("im,pjm->pij", orbitals, half_done, preferred_element_type=jnp.float32)
            .reshape(aux, norb * norb)
            .astype(jnp.bfloat16)
        )
    rows = max(r for r in range(1, 33) if half % r == 0)
    steps = half // rows
    stride = -(-half // SUBLANES) * SUBLANES
    turned = jnp.transpose(integrals, (1, 0, 2))
    return pl.pallas_call(
        functools.partial(transform_kernel, rows=rows, half=half, stride=stride),
        grid=(steps,),
        in_specs=[
            pl.BlockSpec((rows, aux, nbas), lambda s: (s, 0, 0)),
            pl.BlockSpec((rows, aux, nbas), lambda s, steps=steps: (s + steps, 0, 0)),
            pl.BlockSpec((norb, nbas), lambda s: (0, 0)),
        ],
        out_specs=pl.BlockSpec((aux, norb * norb), lambda s: (0, 0)),
        out_shape=jax.ShapeDtypeStruct((aux, norb * norb), jnp.bfloat16),
        scratch_shapes=[
            pltpu.VMEM((PACK * stride, LANES), jnp.float32),
            pltpu.VMEM((norb * PACK, LANES), jnp.float32),
            pltpu.VMEM((aux, norb * norb), jnp.float32),
        ],
        compiler_params=pltpu.CompilerParams(
            dimension_semantics=("arbitrary",), vmem_limit_bytes=40 * 1024 * 1024
        ),
        name="transform",
    )(turned, turned, orbitals)


def alpha_kernel(f_ref, addr_ref, sign_ref, seg_a_ref, seg_b_ref, allowed_ref, h_ref, mask_ref):
    aux, pairs = f_ref.shape
    n_alpha = addr_ref.shape[0]
    blocks = allowed_ref.shape[0]
    side = LANES // aux
    factors = f_ref[...]
    addr = addr_ref[...]
    sign = sign_ref[...].astype(jnp.float32)
    total = None
    for q in range(side):
        hot = [jnp.where(addr == g * side + q, sign, 0.0) for g in range(n_alpha // side)]
        left = jnp.concatenate(hot, axis=0).astype(jnp.bfloat16)
        pieces = []
        if q:
            pieces.append(jnp.zeros((q * aux, pairs), jnp.bfloat16))
        pieces.append(factors)
        if q + 1 < side:
            pieces.append(jnp.zeros((LANES - (q + 1) * aux, pairs), jnp.bfloat16))
        part = lax.dot_general(left, jnp.concatenate(pieces, axis=0), NT, preferred_element_type=jnp.float32)
        total = part if total is None else total + part
    for g in range(n_alpha // side):
        h_ref[:, g * LANES : (g + 1) * LANES] = total[g * n_alpha : (g + 1) * n_alpha, :]
    hot_b = (
        lax.broadcasted_iota(jnp.int32, (blocks, seg_b_ref.shape[1]), 0) == seg_b_ref[...]
    ).astype(jnp.float32)
    hot_a = (lax.broadcasted_iota(jnp.int32, (blocks, n_alpha), 0) == seg_a_ref[...]).astype(jnp.float32)
    columns = jnp.dot(allowed_ref[...].astype(jnp.float32), hot_b, preferred_element_type=jnp.float32)
    mask_ref[...] = lax.dot_general(
        hot_a, columns, (((0,), (0,)), ((), ())), preferred_element_type=jnp.float32
    )


def alpha_side(factors, alpha_addr, alpha_sign, seg_alpha, seg_beta, allowed):
    n_alpha = alpha_addr.shape[0]
    n_beta = seg_beta.shape[0]
    return pl.pallas_call(
        alpha_kernel,
        out_shape=(
            jax.ShapeDtypeStruct((n_alpha, n_alpha * factors.shape[0]), jnp.float32),
            jax.ShapeDtypeStruct((n_alpha, n_beta), jnp.float32),
        ),
        name="alpha_side",
    )(factors, alpha_addr, alpha_sign, seg_alpha.reshape(1, -1), seg_beta.reshape(1, -1), allowed)


def beta_kernel(vec_ref, f_ref, h_ref, mask_ref, addr_ref, sign_ref, out_ref, source_ref, pairs_ref, t_ref, turn_ref):
    aux, pairs = f_ref.shape
    n_alpha, n_beta = mask_ref.shape
    held, padded, _ = pairs_ref.shape
    chunks = n_beta // LANES
    turns = n_alpha // held
    source_ref[...] = (vec_ref[...].astype(jnp.float32) * mask_ref[...]).reshape(turns, held, n_beta)
    if padded != pairs:
        tail = pairs // PACK * PACK
        pairs_ref[:, tail:, :] = jnp.zeros((held, padded - tail, n_beta), jnp.bfloat16)

    def gathered(turn, k, index):
        value = None
        for c in range(chunks):
            row = jnp.broadcast_to(
                source_ref[turn, k : k + 1, c * LANES : (c + 1) * LANES], (index.shape[0], LANES)
            )
            found = jnp.take_along_axis(row, index % LANES if chunks > 1 else index, axis=1, mode="promise_in_bounds")
            value = found if value is None else jnp.where(index // LANES == c, found, value)
        return value

    def fill(turn, start, count):
        for c in range(chunks):
            index = addr_ref[pl.ds(start, count), c * LANES : (c + 1) * LANES]
            sign = sign_ref[pl.ds(start, count), c * LANES : (c + 1) * LANES].astype(jnp.float32)
            for k in range(held):
                pairs_ref[k, pl.ds(start, count), c * LANES : (c + 1) * LANES] = (
                    gathered(turn, k, index) * sign
                ).astype(jnp.bfloat16)

    factors = f_ref[...]

    def run(turn):
        def step(i, carry):
            fill(turn, pl.multiple_of(i * PACK, PACK), PACK)
            return carry

        lax.fori_loop(0, pairs // PACK, step, 0)
        if pairs % PACK:
            fill(turn, pairs // PACK * PACK, pairs % PACK)
        for k in range(held):
            t_ref[turn, k * aux : (k + 1) * aux, :] = jnp.dot(
                factors, pairs_ref[k, :pairs, :], preferred_element_type=jnp.float32
            )

    if turns == 1:
        run(0)
    else:
        pl.loop(0, turns)(run)

    partial = (
        jnp.dot(h_ref[...], t_ref[...].reshape(n_alpha * aux, n_beta), preferred_element_type=jnp.float32, precision=lax.Precision.HIGHEST)
        * mask_ref[...]
    )
    turn_ref[...] = partial.T
    devices = out_ref.shape[0]
    local = n_beta // devices
    out_ref[...] = jnp.concatenate(
        [turn_ref[pl.ds(k, devices, stride=local), :] for k in range(local)], axis=1
    )


def beta_side(vec, factors, h, mask, beta_addr, beta_sign, devices):
    aux, pairs = factors.shape
    n_alpha, n_beta = mask.shape
    padded = -(-pairs // PACK) * PACK
    held = max(k for k in range(1, n_alpha + 1) if n_alpha % k == 0 and k * padded * n_beta * 2 <= 12 * 2**20)
    return pl.pallas_call(
        beta_kernel,
        out_shape=jax.ShapeDtypeStruct((devices, n_beta // devices * n_alpha), jnp.float32),
        scratch_shapes=[
            pltpu.VMEM((n_alpha // held, held, n_beta), jnp.float32),
            pltpu.VMEM((held, padded, n_beta), jnp.bfloat16),
            pltpu.VMEM((n_alpha // held, held * aux, n_beta), jnp.float32),
            pltpu.VMEM((n_beta, n_alpha), jnp.float32),
        ],
        name="beta_side",
    )(vec, factors, h, mask, beta_addr.T, beta_sign.T)


def add_kernel(parts_ref, out_ref):
    total = jnp.sum(parts_ref[...], axis=0, keepdims=True)
    rows, columns = out_ref.shape
    for k in range(rows):
        out_ref[k : k + 1, :] = total[:, k * columns : (k + 1) * columns]


def on_device(
    vector,
    integrals,
    orbitals,
    alpha_addr,
    alpha_sign,
    beta_addr,
    beta_sign,
    seg_alpha,
    seg_beta,
    allowed,
):
    devices = lax.axis_size(AXES)
    n_beta = vector.shape[1]
    n_alpha = alpha_addr.shape[0]
    vec = lax.all_to_all(
        jnp.broadcast_to(vector, (devices,) + vector.shape), AXES, split_axis=0, concat_axis=0, tiled=True
    ).reshape(n_alpha, n_beta)
    factors = transform(integrals, orbitals)
    h, mask = alpha_side(factors, alpha_addr, alpha_sign, seg_alpha, seg_beta, allowed)
    partial = beta_side(vec, factors, h, mask, beta_addr, beta_sign, devices)
    parts = lax.all_to_all(partial, AXES, split_axis=0, concat_axis=0, tiled=True)
    return pl.pallas_call(
        add_kernel,
        out_shape=jax.ShapeDtypeStruct((n_beta // devices, n_alpha), jnp.float32),
        name="add_parts",
    )(parts)


def solution(mesh):
    rows = P(AXES, None)
    placed = (rows, P(AXES, None, None), P(), P(), P(), P(), P(), P(), P(), P())
    return jax.shard_map(on_device, mesh=mesh, in_specs=placed, out_specs=rows, check_vma=False)
```

time: 145 us -> 49.4 us (0.34)
  blocking collectives: 70 us -> 13.1 us
  matrix products: 40.3 us -> 0 us
  Pallas kernels: 0 us -> 25.2 us
  local copies, waits for them, and re-layouts: 19.7 us -> 3.22 us
  between operations: 13.6 us -> 0.04 us
  starting transfers between devices: 0.01 us -> 7.33 us
    all_gather x1 -> x0, blocking collectives: 70 us -> none  [on_device(): whole_t = lax.all_gather(masked_t, ('grp', 'blk'), axis=1, tiled=True)]
    dot_general x32 -> x0, matrix products: 40.3 us -> none  [the longest x1 24 us: on_device(): jnp.einsum('im,pjm->pij', orbitals, half_done, preferred_element_type=jnp...]
    pallas_call x0 -> x4, Pallas kernels: none -> 25.2 us  [the longest x1 12.3 us: transform(): pl.pallas_call(functools.partial(transform_kernel, rows=rows, half=half,...]
    all_to_all x0 -> x1, blocking collectives: none -> 13.1 us  [on_device(): lax.all_to_all(partial, AXES, split_axis=0, concat_axis=0, tiled=True)]
    all_to_all x0 -> x1, starting transfers between devices: none -> 7.33 us  [on_device(): lax.all_to_all(jnp.broadcast_to(vector, (devices,) + vector.shape), AXES,...]
    dynamic_slice x82 -> x0, local copies, waits for them, and re-layouts: 6.54 us -> none  [the longest x78 5.56 us: on_device(): lax.scan(add_block, jnp.zeros((b_cols, n_alpha), jnp.float32), (addr_bloc...]
    gather x3 -> x0, local copies, waits for them, and re-layouts: 6.33 us -> none  [on_device(): jnp.take(whole_t, local_addr.reshape(-1), axis=0)]
    reshape x4 -> x0, local copies, waits for them, and re-layouts: 3.29 us -> none  [the longest x1 2.19 us: on_device(): products.reshape(b_cols, orbital_count, orbital_count, n_alpha)]
  transfers between devices with their start and end apart: 1 -> 1, of which waited for: 0 -> 0; matrix products, arithmetic and copies ran while one was open for 7% -> 0% of each run, Pallas kernels for 0% -> 30%
where the time goes in v1:
time: 49.4 us; the launch traced here: 48.9 us
  Pallas kernels  25.2 us (51%)
  blocking collectives  13.1 us (27%)
  starting transfers between devices  7.33 us (15%)
  local copies, waits for them, and re-layouts  3.22 us (7%)
    all_to_all x1, blocking collectives, on_device(): lax.all_to_all(partial, AXES, split_axis=0, concat_axis=0, tiled=True)  13.1 us
    pallas_call x1, Pallas kernels, transform(): pl.pallas_call(functools.partial(transform_kernel, rows=rows, half=half,...  12.3 us
    pallas_call x1, Pallas kernels, beta_side(): pl.pallas_call(beta_kernel, out_shape=jax.ShapeDtypeStruct((devices, n_be...  9.34 us
    all_to_all x1, starting transfers between devices, on_device(): lax.all_to_all(jnp.broadcast_to(vector, (devices,) + vector.shape), AXES,...  7.33 us
    pallas_call x1, Pallas kernels, alpha_side(): pl.pallas_call(alpha_kernel, out_shape=(jax.ShapeDtypeStruct((n_alpha, n_...  2.25 us
    unnamed x5, local copies, waits for them, and re-layouts  1.97 us
    pallas_call x1, Pallas kernels, on_device(): pl.pallas_call(add_kernel, out_shape=jax.ShapeDtypeStruct((n_beta // devi...  1.37 us
    broadcast_in_dim x1, local copies, waits for them, and re-layouts, on_device(): jnp.broadcast_to(vector, (devices,) + vector.shape)  1.26 us
  transfers between devices with their start and end apart: 1, of which 0 were waited for; matrix products, arithmetic and copies ran while one was open for 0% of the time, Pallas kernels for 30%

profile of v1, /device:TPU:0, one launch (start us, length us, event | category | flops | bytes accessed | tf_op | source)
XLA Modules:
  0.0 48.9 jit_solution(2219642036930448919)
XLA Ops:
  0.0 1.3 %broadcast_in_dim.3 = bf16[32,1,128]{2,1,0:T(2,128)(2,1)} broadcast(bf16[128]{0:T(256)(128)(2,1)} %bitcast.22), dimensions={2} | broadcast | bytes 8448 | tf_op jit(solution)/shard_map/broadcast_in_dim | solution.py:243
  1.3 7.3 %all-to-all-start = ((bf16[32,1,128]{2,1,0:T(2,128)(2,1)}), bf16[32,1,128]{2,1,0:T(2,128)(2,1)S(1)}, u32[]{:S(2)}, u32[]{:S(2)}) async-start(bf16[32,1,128]{2,1,0:T(2,128)(2,1)} %broadcast_in_dim.3), calls=%async_computation | async-start | bytes 32768 | tf_op jit(solution)/shard_map/all_to_all | solution.py:242
  8.6 0.0 copy-start.1
  8.6 0.7 %copy-done.1 = bf16[26,500]{1,0:T(8,128)(2,1)S(1)} copy-done((bf16[26,500]{1,0:T(8,128)(2,1)S(1)}, bf16[26,500]{1,0:T(8,128)(2,1)}, u32[]{:S(2)}) %copy-start.1) | copy-done | bytes 26024
  9.4 12.3 %transform.1.f_ref = bf16[32,676]{1,0:T(8,128)(2,1)S(1)} custom-call(bf16[500,32,500]{2,1,0:T(8,128)(2,1)} %bitcast.13, bf16[500,32,500]{2,1,0:T(8,128)(2,1)} %bitcast.14, bf16[26,500]{1,0:T(8,128)(2,1)S(1)} %copy-done.1), custom_call_target="tpu_custom_call" | custom-call | tf_op jit(solution)/shard_map/transform/pallas_call | solution.py:73
  21.6 0.0 copy-start
  21.6 0.6 %copy-done = bf16[32,676]{1,0:T(8,128)(2,1)} copy-done((bf16[32,676]{1,0:T(8,128)(2,1)}, bf16[32,676]{1,0:T(8,128)(2,1)S(1)}, u32[]{:S(2)}) %copy-start) | copy-done | bytes 43288
  22.2 2.3 %alpha_side.1 = (f32[32,1024]{1,0:T(8,128)}, f32[32,128]{1,0:T(8,128)}) custom-call(bf16[32,676]{1,0:T(8,128)(2,1)} %copy-done, s32[32,676]{1,0:T(8,128)} %addr_ref.1, s32[32,676]{1,0:T(8,128)} %sign_ref.1, s32[1,32]{1,0:T(1,128)} %bitcast.20, s32[1,128]{1,0:T(1,128)} %bitcast.21, s32[10,10]{1,0:T(8,128)} %allowed_ref.1), custom_call_target="tpu_custom_call" | custom-call | tf_op jit(solution)/shard_map/alpha_side/pallas_call | solution.py:130
  24.5 0.0 all-to-all-done
  24.5 0.6 %copy.15 = bf16[32,1,128]{2,0,1:T(8,128)(2,1)} copy(bf16[32,1,128]{2,1,0:T(2,128)(2,1)S(1)} %all-to-all-done) | data formatting | bytes 16384
  25.1 9.3 %beta_side.1 = f32[32,128]{1,0:T(8,128)} custom-call(bf16[32,128]{1,0:T(8,128)(2,1)} %bitcast.19, bf16[32,676]{1,0:T(8,128)(2,1)} %copy-done, f32[32,1024]{1,0:T(8,128)} %get-tuple-element.7.h_ref, f32[32,128]{1,0:T(8,128)} %get-tuple-element.8.mask_ref, s32[676,128]{1,0:T(8,128)} %bitcast.15, s32[676,128]{1,0:T(8,128)} %bitcast.16), custom_call_target="tpu_custom_call" | custom-call | tf_op jit(solution)/shard_map/beta_side/pallas_call | solution.py:207
  34.4 13.1 %all_to_all.16 = f32[32,1,128]{2,1,0:T(1,128)} all-to-all(f32[32,1,128]{2,1,0:T(1,128)} %bitcast.17), channel_id=1, replica_groups=mesh['grp'=4,'blk'=8] {'grp','blk'}, dimensions={0} | all-to-all | bytes 32768 | tf_op jit(solution)/shard_map/all_to_all | solution.py:248
  47.5 1.4 %add_parts.1 = f32[4,32]{1,0:T(4,128)} custom-call(f32[32,128]{1,0:T(8,128)} %bitcast.18), custom_call_target="tpu_custom_call" | custom-call | tf_op jit(solution)/shard_map/add_parts/pallas_call | solution.py:249
Async XLA Ops:
  1.3 23.2 %all-to-all-start = ((bf16[32,1,128]{2,1,0:T(2,128)(2,1)}), bf16[32,1,128]{2,1,0:T(2,128)(2,1)S(1)}, u32[]{:S(2)}, u32[]{:S(2)}) async-start(bf16[32,1,128]{2,1,0:T(2,128)(2,1)} %broadcast_in_dim.3), calls=%async_computation | async-start | bytes 32768 | tf_op jit(solution)/shard_map/all_to_all | solution.py:242
  8.6 0.8 %copy-start.1 = (bf16[26,500]{1,0:T(8,128)(2,1)S(1)}, bf16[26,500]{1,0:T(8,128)(2,1)}, u32[]{:S(2)}) copy-start(bf16[26,500]{1,0:T(8,128)(2,1)} %orb_ref.1) | copy-start | bytes 78004
  21.6 0.6 %copy-start = (bf16[32,676]{1,0:T(8,128)(2,1)}, bf16[32,676]{1,0:T(8,128)(2,1)S(1)}, u32[]{:S(2)}) copy-start(bf16[32,676]{1,0:T(8,128)(2,1)S(1)} %transform.1.f_ref) | copy-start | bytes 129796
